TPU v7x, 512 devices: a whole 4x8x8 slice. The times are simulated.
512 devices in a mesh: boxes: 128 (over y, z, core), probe: 4 (over x).
Axes of the slice: x: 4, y: 8, z: 8, core: 2. Of those that a mesh axis runs over, the one named last changes fastest.
Arguments:
- probes: float32 [32, 1048576], P('probe', 'boxes'), may hold values from -0.3 to 0.3
- points: float32 [3, 1048576], P(None, 'boxes'), may hold values from -1 to 1, as said below
- near_list: int32 [4096, 6], P('boxes'), may hold values from -1 to 4095, as said below
- leaf_proxy: float32 [3, 262144], P(None, 'boxes'), may hold values from -1 to 1, as said below
- inner_proxy: float32 [3, 245760], P(None, 'boxes'), may hold values from -1 to 1, as said below
- top_proxy: float32 [3, 16128], replicated, may hold values from -1 to 1, as said below
- far_list: int32 [4096, 3], P('boxes'), may hold values from -1 to 4095, as said below
Outputs:
- kernel_product: float32 [32, 1048576], P('probe', 'boxes')
Inputs may be any that keep to these rules, and one draw needn't show every extreme that they name: `points`: points on the unit sphere, box by box along a curve over it. `leaf_proxy`: proxy points on the unit sphere. `inner_proxy`: proxy points on the unit sphere. `top_proxy`: proxy points on the unit sphere. `near_list`: row b holds b - 1, b, b + 1 (modulo 4096) and those of the three candidates of row b of far_list that are -1 there, in some order, live entries first, then -1; some row is full. `far_list`: in row b, slot 0 holds b - 2, slot 1 holds b + 2, slot 2 holds b + 3 for even b and b - 3 for odd b (all modulo 4096), or -1.
All inputs are finite; a program needn't handle non-finite values.
Results may differ from a plain program's by a relative error of at most 0.00013.
Values sent between devices are 32-bit elements; how exact they have to be, the bound alone decides.
A program may use at most 64 MiB of HBM per device.

v0:
```python
import jax
import jax.numpy as jnp
from jax import lax
from jax.sharding import PartitionSpec as P

BOXES_DEV = 32
P_SIZE = 256
R = 64
W = 3
INNER_DEV = 30
SHARPNESS = 0.05
NUGGET = 1.0
PRECISE = lax.Precision.HIGHEST


def with_halo(array, sides, width):
    for axis, dim in sides:
        size, length = (lax.axis_size(axis), array.shape[dim])
        up = [(i, (i + 1) % size) for i in range(size)]
        down = [(j, i) for i, j in up]
        last = lax.slice_in_dim(array, length - width, length, axis=dim)
        initial = lax.slice_in_dim(array, 0, width, axis=dim)
        before = lax.ppermute(last, axis, up)
        after = lax.ppermute(initial, axis, down)
        array = jnp.concatenate([before, array, after], axis=dim)
    return array


def kernel_matrix(left_points, right_points, kernel_scale):
    distance_sq = (left_points[0][..., :, None] - right_points[0][..., None, :]) ** 2
    distance_sq = distance_sq + (left_points[1][..., :, None] - right_points[1][..., None, :]) ** 2
    distance_sq = distance_sq + (left_points[2][..., :, None] - right_points[2][..., None, :]) ** 2
    return 1.0 / (1.0 + kernel_scale * distance_sq)


def interpolation(left_points, right_points, kernel_scale):
    values = kernel_matrix(left_points, right_points, kernel_scale)
    return values / jnp.sum(values, axis=-1, keepdims=True)


def body(probes, points, near_list, leaf_proxy, inner_proxy, top_proxy, far_list):
    groups = lax.axis_size("boxes")
    device = lax.axis_index("boxes")
    boxes_all = BOXES_DEV * groups
    kernel_scale = SHARPNESS * boxes_all
    rows_here = probes.shape[0]
    local_depth = BOXES_DEV.bit_length() - 1
    tree_depth = groups.bit_length() - 1
    live_slot = near_list >= 0
    slot_weight = live_slot.astype(jnp.float32)
    where_in = jnp.where(live_slot, (near_list - device * BOXES_DEV + W + boxes_all) % boxes_all, 0)
    box_points = points.reshape(3, BOXES_DEV, P_SIZE)
    stacked = jnp.concatenate([probes, points], axis=0)
    extended = with_halo(stacked, (("boxes", 1),), W * P_SIZE)
    extended = extended.reshape(rows_here + 3, BOXES_DEV + 2 * W, P_SIZE)

    def near_box(near_inputs):
        slot_index, slot_mask, targets = near_inputs
        near_tiles = jnp.take(extended, slot_index, axis=1)
        near_values = near_tiles[:rows_here] * slot_mask[None, :, None]
        kernel_block = kernel_matrix(near_tiles[rows_here:], targets[:, None, :], kernel_scale)
        return jnp.einsum("qns,nst->qt", near_values, kernel_block, precision=PRECISE)

    near_field = lax.map(near_box, (where_in, slot_weight, jnp.moveaxis(box_points, 1, 0)))
    near_field = jnp.moveaxis(near_field, 0, 1).reshape(rows_here, BOXES_DEV * P_SIZE)
    probe_tiles = probes.reshape(rows_here, BOXES_DEV, P_SIZE)
    leaf_points = leaf_proxy.reshape(3, BOXES_DEV, R)
    leaf_basis = interpolation(box_points, leaf_points, kernel_scale)
    inner_points = inner_proxy.reshape(3, INNER_DEV, R)
    top_points = top_proxy.reshape(3, top_proxy.shape[1] // R, R)

    def node_proxy(height, node_index):
        offset = 2 * groups - 2 * (groups >> height)
        return lax.dynamic_slice_in_dim(top_points, offset + node_index, 1, 1)

    proxies = [leaf_points]
    for height in range(1, local_depth):
        offset = BOXES_DEV - (BOXES_DEV >> height - 1)
        number = BOXES_DEV >> height
        proxies.append(inner_points[:, offset : offset + number, :])
    proxies.append(node_proxy(0, device))
    level_moments = [jnp.einsum("qbp,bpr->qbr", probe_tiles, leaf_basis, precision=PRECISE)]
    transfer_maps = []
    for height in range(local_depth):
        interp_map = interpolation(
            proxies[height], jnp.repeat(proxies[height + 1], 2, axis=1), kernel_scale
        )
        transfer_maps.append(interp_map)
        lifted = jnp.einsum("qnr,nrs->qns", level_moments[-1], interp_map, precision=PRECISE)
        level_moments.append(lifted.reshape(rows_here, -1, 2, R).sum(axis=2))
    pyramid = jnp.concatenate(
        [
            jnp.concatenate(level_moments[:local_depth], axis=1),
            jnp.concatenate([leaf_points, inner_points], axis=1),
        ],
        axis=0,
    )
    pyramid_nodes = pyramid.shape[1]
    spread = with_halo(pyramid, (("boxes", 1),), pyramid_nodes)
    local_couplings = []
    for height in range(local_depth):
        count = BOXES_DEV >> height
        start = 0 if height == 0 else 2 * BOXES_DEV - (BOXES_DEV >> height - 1)
        view = jnp.concatenate(
            [
                spread[:, block * pyramid_nodes + start : block * pyramid_nodes + start + count, :]
                for block in range(3)
            ],
            axis=1,
        )
        if height == 0:
            live_far = far_list >= 0
            slot_ids = [
                jnp.where(
                    live_far[:, slot],
                    (far_list[:, slot] - device * BOXES_DEV + BOXES_DEV + boxes_all) % boxes_all,
                    0,
                )
                for slot in range(3)
            ]
            slot_masks = [live_far[:, slot].astype(jnp.float32)[None, :, None] for slot in range(3)]
        else:
            node = jnp.arange(count, dtype=jnp.int32)
            third = jnp.where(node % 2 == 0, node + 3, node - 3)
            slot_ids = [node - 2 + count, node + 2 + count, third + count]
            slot_masks = [None, None, None]
        coupling = jnp.zeros((rows_here, count, R), jnp.float32)
        for slot in range(3):
            picked = jnp.take(view, slot_ids[slot], axis=1)
            kernel_block = kernel_matrix(picked[rows_here:], proxies[height], kernel_scale)
            source_moment = picked[:rows_here]
            if slot_masks[slot] is not None:
                source_moment = source_moment * slot_masks[slot]
            coupling = coupling + jnp.einsum(
                "qnr,nrs->qns", source_moment, kernel_block, precision=PRECISE
            )
        local_couplings.append(coupling)
    top_levels = tree_depth - 1
    level_points = []
    for height in range(top_levels):
        offset = 2 * groups - 2 * (groups >> height)
        level_points.append(top_points[:, offset : offset + (groups >> height), :])
    level_moments_top = [lax.all_gather(level_moments[local_depth], "boxes", axis=1, tiled=True)]
    edge_maps = []
    for height in range(top_levels - 1):
        interp_map = interpolation(
            level_points[height], jnp.repeat(level_points[height + 1], 2, axis=1), kernel_scale
        )
        edge_maps.append(interp_map)
        lifted = jnp.einsum("qnr,nrs->qns", level_moments_top[-1], interp_map, precision=PRECISE)
        level_moments_top.append(lifted.reshape(rows_here, -1, 2, R).sum(axis=2))
    top_couplings = []
    for height in range(top_levels):
        number = groups >> height
        node = device // 2**height
        third = jnp.where(node % 2 == 0, node + 3, node - 3) % number
        if number > 4:
            source_ids = [(node - 2) % number, (node + 2) % number, third]
        else:
            source_ids = [(node + 2) % number]
        target_points = lax.dynamic_slice_in_dim(level_points[height], node, 1, 1)
        coupling = jnp.zeros((rows_here, 1, R), jnp.float32)
        for source in source_ids:
            kernel_block = kernel_matrix(
                lax.dynamic_slice_in_dim(level_points[height], source, 1, 1),
                target_points,
                kernel_scale,
            )
            source_moment = lax.dynamic_slice_in_dim(level_moments_top[height], source, 1, 1)
            coupling = coupling + jnp.einsum(
                "qnr,nrs->qns", source_moment, kernel_block, precision=PRECISE
            )
        top_couplings.append(coupling)
    descent = top_couplings[-1]
    for height in range(top_levels - 2, -1, -1):
        own_edge = lax.dynamic_slice_in_dim(edge_maps[height], device // 2**height, 1, 0)
        descent = (
            jnp.einsum("qns,nrs->qnr", descent, own_edge, precision=PRECISE) + top_couplings[height]
        )
    for height in range(local_depth - 1, -1, -1):
        descent = jnp.einsum(
            "qns,nrs->qnr", jnp.repeat(descent, 2, axis=1), transfer_maps[height], precision=PRECISE
        )
        descent = descent + local_couplings[height]
    far_field = jnp.einsum("qbr,bpr->qbp", descent, leaf_basis, precision=PRECISE).reshape(
        rows_here, BOXES_DEV * P_SIZE
    )
    return near_field + far_field + NUGGET * probes


def solution(mesh):
    in_specs = (
        P("probe", "boxes"),
        P(None, "boxes"),
        P("boxes", None),
        P(None, "boxes"),
        P(None, "boxes"),
        P(),
        P("boxes", None),
    )
    out_specs = P("probe", "boxes")
    return jax.shard_map(body, mesh=mesh, in_specs=in_specs, out_specs=out_specs, check_vma=False)
```

profile of v0, /device:TPU:1, one launch (start us, length us, event | category | flops | bytes accessed | tf_op | source)
XLA Modules:
  0.0 403.7 jit_solution(18085279957621713053)
XLA Ops:
  5.6 3.8 constant_dynamic-update-slice_fusion.6
  11.0 2.6 bitcast_reduce_fusion.3
  18.6 8.8 %collective-permute-start.3 = (f32[11,62,64]{2,0,1:T(8,128)S(1)}, f32[11,62,64]{2,0,1:T(8,128)}, u32[]{:S(2)}, u32[]{:S(2)}) collective-permute-start(f32[11,62,64]{2,0,1:T(8,128)S(1)} %maximum_maximum_fusion), channel_id=1, source_target_pairs={{4,0},{8,4},{12,8},{16,12},{20,16},{24,20},{28,24},{32,28},{36,32}... | collective-permute-start | bytes 523784 | tf_op jit(solution)/shard_map/ppermute | solution.py:24
  32.0 7.9 %collective-permute-start.1 = (f32[11,768]{1,0:T(8,128)}, f32[11,768]{1,0:T(8,128)}, u32[]{:S(2)}, u32[]{:S(2)}) collective-permute-start(f32[11,768]{1,0:T(8,128)} %get-tuple-element.106), channel_id=1, source_target_pairs={{4,0},{8,4},{12,8},{16,12},{20,16},{24,20},{28,24},{32,28},{36,32}... | collective-permute-start | bytes 101384 | tf_op jit(solution)/shard_map/ppermute | solution.py:24
  58.8 52.1 %all-gather.1 = f32[128,64,8]{1,2,0:T(8,128)S(1)} all-gather(f32[1,64,8]{1,2,0:T(8,128)S(1)} %convolution_bitcast_fusion.3), channel_id=2, replica_groups=mesh['boxes'=128,'probe'=4] {'boxes'}, dimensions={0}, use_global_device_ids=true | all-gather | bytes 264192 | tf_op jit(solution)/shard_map/all_gather | solution.py:143
  111.5 5.6 %divide_reduce_fusion = f32[128,64]{1,0:T(8,128)S(1)} fusion(f32[128,64]{1,0:T(8,128)S(1)} %bitcast.618, f32[128,64]{1,0:T(8,128)S(1)} %get-tuple-element.123, f32[128,64]{1,0:T(8,128)S(1)} %bitcast.621, f32[128,64]{1,0:T(8,128)S(1)} %get-tuple-element.124, f32[128,64]{1,0:T(8,128)S(1)} %bitcast.615, f32[128,64]{1,0:T(8,128)S(1)} %get-tuple-element.122), kind=kLoop, calls=%fused_computation.49 | loop fusion | flops 6283264 | bytes 229376 | tf_op jit(solution)/shard_map/reduce_sum | solution.py:38
  117.1 6.3 %multiply_divide_fusion = f32[128,64,64]{2,1,0:T(8,128)} fusion(f32[128,64]{1,0:T(8,128)S(1)} %divide_reduce_fusion, f32[128,64]{1,0:T(8,128)S(1)} %bitcast.619, f32[128,64]{1,0:T(8,128)S(1)} %get-tuple-element.123, f32[128,64]{1,0:T(8,128)S(1)} %bitcast.622, f32[128,64]{1,0:T(8,128)S(1)} %get-tuple-element.124, f32[128,64]{1,0:T(8,128)S(1)} %bitcast.616, ...), kind=kLoop, calls=%fused_computation.47 | loop fusion | flops 6291456 | bytes 2326528 | tf_op jit(solution)/shard_map/div | solution.py:38
  123.4 10.2 %bitcast_reduce_fusion = f32[8,64,64]{2,0,1:T(8,128)S(1)} fusion(f32[8,128,64]{2,1,0:T(8,128)S(1)} %reshape.5058, f32[128,64]{1,0:T(8,128)S(1)} %divide_reduce_fusion, f32[128,64]{1,0:T(8,128)S(1)} %bitcast.620, f32[128,64]{1,0:T(8,128)S(1)} %get-tuple-element.123, f32[128,64]{1,0:T(8,128)S(1)} %bitcast.623, f32[128,64]{1,0:T(8,128)S(1)} %get-tuple-element.124, ...), kind=kOutput, calls=%fused_computation.131 | convolution fusion | flops 56655872 | bytes 622592 | tf_op jit(solution)/shard_map/qnr,nrs->qns/dot_general | solution.py:150
  133.8 2.7 divide_reduce_fusion.1
  136.5 3.1 multiply_divide_fusion.1
  139.7 5.1 %bitcast_reduce_fusion.1 = f32[8,32,64]{2,0,1:T(8,128)S(1)} fusion(f32[8,64,64]{2,0,1:T(8,128)S(1)} %bitcast_reduce_fusion, f32[64,64]{1,0:T(8,128)S(1)} %divide_reduce_fusion.1, f32[64,64]{1,0:T(8,128)S(1)} %bitcast.630, f32[64,64]{1,0:T(8,128)S(1)} %copy-done.5, f32[64,64]{1,0:T(8,128)S(1)} %bitcast.633, f32[64,64]{1,0:T(8,128)S(1)} %copy-done.7, ...), kind=kOutput, calls=%fused_computation.189 | convolution fusion | flops 28327936 | bytes 311296 | tf_op jit(solution)/shard_map/qnr,nrs->qns/dot_general | solution.py:150
  148.4 2.6 bitcast_reduce_fusion.2
  176.6 182.3 %while.10 = (s32[]{:T(128)}, f32[32,8,256]{2,1,0:T(8,128)}, s32[32,6]{1,0:T(8,128)}, f32[11,38,256]{2,0,1:T(8,128)S(1)}, f32[32,6]{1,0:T(8,128)}, /*index=5*/f32...) while((s32[]{:T(128)}, f32[32,8,256]{2,1,0:T(8,128)}, s32[32,6]{1,0:T(8,128)}, ...), condition=%wide.region_1.2_spmd, body=%wide.region_0.1_spmd.sunk | while | flops 42104376 | bytes 440149 | solution.py:64
  180.2 2.2 fusion.862
  185.8 2.2 fusion.862
  191.5 2.2 fusion.862
  197.2 2.2 fusion.862
  202.8 2.2 fusion.862
  208.5 2.2 fusion.862
  237.0 2.2 fusion.862
  259.8 2.2 fusion.862
  294.0 2.2 fusion.862
  299.7 2.2 fusion.862
  305.4 2.2 fusion.862
  311.1 2.2 fusion.862
  328.2 2.2 fusion.862
  356.7 2.2 fusion.862
  388.6 2.3 fusion.54
  390.9 2.3 convolution_add_fusion.1
  393.3 2.3 convolution_add_fusion
  396.9 3.2 fusion.17
  400.2 2.7 fusion.16
  (856 shorter events, 245.3 us)
Async XLA Ops:
  0.9 56.1 %copy-start.82 = (f32[2,64]{1,0:T(2,128)}, f32[2,64]{1,0:T(2,128)S(1)}, u32[]{:S(2)}) copy-start(f32[2,64]{1,0:T(2,128)S(1)} %get-tuple-element.194) | copy-start | bytes 1540
  0.9 56.1 %copy-start.84 = (f32[2,64]{1,0:T(2,128)}, f32[2,64]{1,0:T(2,128)S(1)}, u32[]{:S(2)}) copy-start(f32[2,64]{1,0:T(2,128)S(1)} %get-tuple-element.195) | copy-start | bytes 1540
  0.9 56.1 %copy-start.86 = (f32[2,64]{1,0:T(2,128)}, f32[2,64]{1,0:T(2,128)S(1)}, u32[]{:S(2)}) copy-start(f32[2,64]{1,0:T(2,128)S(1)} %get-tuple-element.196) | copy-start | bytes 1540
  17.6 28.4 %copy-start.96 = (s32[32,3]{0,1:T(4,128)S(1)}, s32[32,3]{0,1:T(4,128)}, u32[]{:S(2)}) copy-start(s32[32,3]{0,1:T(4,128)} %param.25) | copy-start | bytes 1156
  17.6 29.7 %copy-start.97 = (s32[32,6]{0,1:T(8,128)S(1)}, s32[32,6]{0,1:T(8,128)}, u32[]{:S(2)}) copy-start(s32[32,6]{0,1:T(8,128)} %param.21) | copy-start | bytes 2308
  17.6 31.0 %copy-start.15 = (f32[3,16128]{1,0:T(4,128)S(1)}, f32[3,16128]{1,0:T(4,128)}, u32[]{:S(2)}) copy-start(f32[3,16128]{1,0:T(4,128)} %param.24) | copy-start | bytes 580612
  17.6 30.3 %copy-start.90 = (f32[2,2,64]{2,1,0:T(2,128)}, f32[2,2,64]{2,1,0:T(2,128)S(1)}, u32[]{:S(2)}) copy-start(f32[2,2,64]{2,1,0:T(2,128)S(1)} %broadcast_in_dim.234) | copy-start | bytes 3076
  17.7 30.3 %copy-start.92 = (f32[2,2,64]{2,1,0:T(2,128)}, f32[2,2,64]{2,1,0:T(2,128)S(1)}, u32[]{:S(2)}) copy-start(f32[2,2,64]{2,1,0:T(2,128)S(1)} %broadcast_in_dim.238) | copy-start | bytes 3076
  17.7 30.3 %copy-start.94 = (f32[2,2,64]{2,1,0:T(2,128)}, f32[2,2,64]{2,1,0:T(2,128)S(1)}, u32[]{:S(2)}) copy-start(f32[2,2,64]{2,1,0:T(2,128)S(1)} %broadcast_in_dim.236) | copy-start | bytes 3076
  18.6 340.3 %collective-permute-start.3 = (f32[11,62,64]{2,0,1:T(8,128)S(1)}, f32[11,62,64]{2,0,1:T(8,128)}, u32[]{:S(2)}, u32[]{:S(2)}) collective-permute-start(f32[11,62,64]{2,0,1:T(8,128)S(1)} %maximum_maximum_fusion), channel_id=1, source_target_pairs={{4,0},{8,4},{12,8},{16,12},{20,16},{24,20},{28,24},{32,28},{36,32}... | collective-permute-start | bytes 523784 | tf_op jit(solution)/shard_map/ppermute | solution.py:24
  27.4 332.2 %collective-permute-start.2 = (f32[11,62,64]{2,0,1:T(8,128)S(1)}, f32[11,62,64]{2,0,1:T(8,128)}, u32[]{:S(2)}, u32[]{:S(2)}) collective-permute-start(f32[11,62,64]{2,0,1:T(8,128)S(1)} %maximum_maximum_fusion), channel_id=1, source_target_pairs={{0,4},{4,8},{8,12},{12,16},{16,20},{20,24},{24,28},{28,32},{32,36}... | collective-permute-start | bytes 523784 | tf_op jit(solution)/shard_map/ppermute | solution.py:23
  30.1 145.3 %collective-permute-start = (f32[11,768]{1,0:T(8,128)}, f32[11,768]{1,0:T(8,128)}, u32[]{:S(2)}, u32[]{:S(2)}) collective-permute-start(f32[11,768]{1,0:T(8,128)} %get-tuple-element.105), channel_id=1, source_target_pairs={{0,4},{4,8},{8,12},{12,16},{16,20},{20,24},{24,28},{28,32},{32,36}... | collective-permute-start | bytes 101384 | tf_op jit(solution)/shard_map/ppermute | solution.py:23
  32.0 143.4 %collective-permute-start.1 = (f32[11,768]{1,0:T(8,128)}, f32[11,768]{1,0:T(8,128)}, u32[]{:S(2)}, u32[]{:S(2)}) collective-permute-start(f32[11,768]{1,0:T(8,128)} %get-tuple-element.106), channel_id=1, source_target_pairs={{4,0},{8,4},{12,8},{16,12},{20,16},{24,20},{28,24},{32,28},{36,32}... | collective-permute-start | bytes 101384 | tf_op jit(solution)/shard_map/ppermute | solution.py:24
  48.8 62.4 %copy-start = (f32[3,252,64]{2,1,0:T(8,128)}, f32[3,252,64]{2,1,0:T(8,128)S(1)}, u32[]{:S(2)}) copy-start(f32[3,252,64]{2,1,0:T(8,128)S(1)} %reshape.4884) | copy-start | bytes 580612
  50.1 83.6 %copy-start.9 = (f32[32,64]{1,0:T(8,128)}, f32[32,64]{1,0:T(8,128)S(1)}, u32[]{:S(2)}) copy-start(f32[32,64]{1,0:T(8,128)S(1)} %get-tuple-element.119) | copy-start | bytes 24580
  50.1 83.6 %copy-start.11 = (f32[32,64]{1,0:T(8,128)}, f32[32,64]{1,0:T(8,128)S(1)}, u32[]{:S(2)}) copy-start(f32[32,64]{1,0:T(8,128)S(1)} %get-tuple-element.120) | copy-start | bytes 24580
  50.1 83.7 %copy-start.13 = (f32[32,64]{1,0:T(8,128)}, f32[32,64]{1,0:T(8,128)S(1)}, u32[]{:S(2)}) copy-start(f32[32,64]{1,0:T(8,128)S(1)} %get-tuple-element.121) | copy-start | bytes 24580
  50.1 83.7 %copy-start.4 = (f32[64,64]{1,0:T(8,128)}, f32[64,64]{1,0:T(8,128)S(1)}, u32[]{:S(2)}) copy-start(f32[64,64]{1,0:T(8,128)S(1)} %get-tuple-element.126) | copy-start | bytes 49156
  50.1 83.7 %copy-start.6 = (f32[64,64]{1,0:T(8,128)}, f32[64,64]{1,0:T(8,128)S(1)}, u32[]{:S(2)}) copy-start(f32[64,64]{1,0:T(8,128)S(1)} %get-tuple-element.127) | copy-start | bytes 49156
  156.3 18.5 %copy-start.85 = (f32[2,64]{1,0:T(2,128)S(1)}, f32[2,64]{1,0:T(2,128)}, u32[]{:S(2)}) copy-start(f32[2,64]{1,0:T(2,128)} %copy-done.84) | copy-start | bytes 1540
  156.3 18.6 %copy-start.87 = (f32[2,64]{1,0:T(2,128)S(1)}, f32[2,64]{1,0:T(2,128)}, u32[]{:S(2)}) copy-start(f32[2,64]{1,0:T(2,128)} %copy-done.86) | copy-start | bytes 1540
  156.3 18.6 %copy-start.107 = (f32[64]{0:T(128)S(1)}, f32[64]{0:T(128)}, u32[]{:S(2)}) copy-start(f32[64]{0:T(128)} %copy-done.106) | copy-start | bytes 772
  156.3 18.6 %copy-start.109 = (f32[64]{0:T(128)S(1)}, f32[64]{0:T(128)}, u32[]{:S(2)}) copy-start(f32[64]{0:T(128)} %copy-done.108) | copy-start | bytes 772
  156.3 18.6 %copy-start.111 = (f32[64]{0:T(128)S(1)}, f32[64]{0:T(128)}, u32[]{:S(2)}) copy-start(f32[64]{0:T(128)} %copy-done.110) | copy-start | bytes 772
  156.3 18.6 %copy-start.113 = (f32[2,64]{1,0:T(2,128)S(1)}, f32[2,64]{1,0:T(2,128)}, u32[]{:S(2)}) copy-start(f32[2,64]{1,0:T(2,128)} %copy-done.112) | copy-start | bytes 1540
  176.6 184.5 %copy-start.124 = (pred[2]{0:T(512)(128)(4,1)S(1)}, pred[2]{0:T(512)(128)(4,1)}, u32[]{:S(2)}) copy-start(pred[2]{0:T(512)(128)(4,1)} %get-tuple-element.277) | copy-start | bytes 10
  176.6 185.9 %copy-start.123 = (pred[2]{0:T(512)(128)(4,1)S(1)}, pred[2]{0:T(512)(128)(4,1)}, u32[]{:S(2)}) copy-start(pred[2]{0:T(512)(128)(4,1)} %get-tuple-element.278) | copy-start | bytes 10
  176.6 186.0 %copy-start.122 = (pred[2]{0:T(512)(128)(4,1)S(1)}, pred[2]{0:T(512)(128)(4,1)}, u32[]{:S(2)}) copy-start(pred[2]{0:T(512)(128)(4,1)} %broadcast_compare_fusion.2) | copy-start | bytes 10
  176.6 188.3 %copy-start.121 = (pred[4]{0:T(512)(128)(4,1)S(1)}, pred[4]{0:T(512)(128)(4,1)}, u32[]{:S(2)}) copy-start(pred[4]{0:T(512)(128)(4,1)} %get-tuple-element.275) | copy-start | bytes 16
  176.6 189.6 %copy-start.120 = (pred[4]{0:T(512)(128)(4,1)S(1)}, pred[4]{0:T(512)(128)(4,1)}, u32[]{:S(2)}) copy-start(pred[4]{0:T(512)(128)(4,1)} %get-tuple-element.276) | copy-start | bytes 16
  176.6 189.7 %copy-start.119 = (pred[4]{0:T(512)(128)(4,1)S(1)}, pred[4]{0:T(512)(128)(4,1)}, u32[]{:S(2)}) copy-start(pred[4]{0:T(512)(128)(4,1)} %compare_and_fusion.12) | copy-start | bytes 16
  176.6 192.2 %copy-start.118 = (pred[8]{0:T(512)(128)(4,1)S(1)}, pred[8]{0:T(512)(128)(4,1)}, u32[]{:S(2)}) copy-start(pred[8]{0:T(512)(128)(4,1)} %get-tuple-element.273) | copy-start | bytes 28
  (113 other events, 613.2 us)
where the time goes:
time: 410 us; the launch traced here: 404 us
  matrix products  138 us (34%)
  local copies, waits for them, and re-layouts  95.9 us (23%)
  other arithmetic  92.4 us (23%)
  blocking collectives  52.1 us (13%)
  starting transfers between devices  20.5 us (5%)
    dot_general x32, matrix products, near_box(): jnp.einsum('qns,nst->qt', near_values, kernel_block, precision=PRECISE)  68.9 us
    all_gather x1, blocking collectives, body(): lax.all_gather(level_moments[local_depth], 'boxes', axis=1, tiled=True)  52.1 us
    slice x42, local copies, waits for them, and re-layouts, kernel_matrix(): right_points[0][..., None, :]  27.3 us
    dot_general x31, matrix products, body(): jnp.einsum('qnr,nrs->qns', source_moment, kernel_block, precision=PRECISE)  26.9 us
    select_n x64, other arithmetic, near_box(): near_tiles = jnp.take(extended, slot_index, axis=1)  24.3 us
    and x32, other arithmetic, near_box(): near_tiles = jnp.take(extended, slot_index, axis=1)  21.9 us
    mul x32, local copies, waits for them, and re-layouts, near_box(): near_values = near_tiles[:rows_here] * slot_mask[None, :, None]  21.8 us
    dot_general x5, matrix products, body(): jnp.einsum('qnr,nrs->qns', level_moments_top[-1], interp_map, precision=P...  20.4 us
  transfers between devices with their start and end apart: 4, of which 0 were waited for; matrix products, arithmetic and copies ran while one was open for 66% of the time, Pallas kernels for 0%

commit v1 on v0

--- a/solution.py
+++ b/solution.py
@@ -140,7 +140,14 @@
     for height in range(top_levels):
         offset = 2 * groups - 2 * (groups >> height)
         level_points.append(top_points[:, offset : offset + (groups >> height), :])
-    level_moments_top = [lax.all_gather(level_moments[local_depth], "boxes", axis=1, tiled=True)]
+    level_moments_top = [
+        jnp.concatenate(
+            lax.all_to_all(
+                jnp.stack([level_moments[local_depth]] * lax.axis_size("boxes")), "boxes", 0, 0
+            ),
+            axis=1,
+        )
+    ]
     edge_maps = []
     for height in range(top_levels - 1):
         interp_map = interpolation(

time: 410 us -> 472 us (1.15)
  the two profiles are of different devices: /device:TPU:1 before, /device:TPU:6 now
where the time goes in v1:
time: 472 us; the launch traced here: 465 us
  matrix products  165 us (35%)
  local copies, waits for them, and re-layouts  153 us (32%)
  other arithmetic  106 us (22%)
  starting transfers between devices  34.5 us (7%)
  between operations  4.88 us (1%)
    dot_general x32, matrix products, near_box(): jnp.einsum('qns,nst->qt', near_values, kernel_block, precision=PRECISE)  90.9 us
    slice x42, local copies, waits for them, and re-layouts, kernel_matrix(): right_points[0][..., None, :]  45.5 us
    mul x32, local copies, waits for them, and re-layouts, near_box(): near_values = near_tiles[:rows_here] * slot_mask[None, :, None]  40.1 us
    dot_general x31, matrix products, body(): jnp.einsum('qnr,nrs->qns', source_moment, kernel_block, precision=PRECISE)  31.7 us
    select_n x64, other arithmetic, near_box(): near_tiles = jnp.take(extended, slot_index, axis=1)  24.4 us
    and x32, other arithmetic, near_box(): near_tiles = jnp.take(extended, slot_index, axis=1)  22 us
    dot_general x5, matrix products, body(): jnp.einsum('qnr,nrs->qns', level_moments_top[-1], interp_map, precision=P...  20.7 us
    ppermute x2, starting transfers between devices, with_halo(): after = lax.ppermute(initial, axis, down)  20.4 us
  transfers between devices with their start and end apart: 5, of which 0 were waited for; matrix products, arithmetic and copies ran while one was open for 75% of the time, Pallas kernels for 0%

profile of v1, /device:TPU:6, one launch (start us, length us, event | category | flops | bytes accessed | tf_op | source)
XLA Modules:
  0.0 465.4 jit_solution(11694956248658193939)
XLA Ops:
  5.6 3.8 constant_dynamic-update-slice_fusion.6
  17.7 13.4 %collective-permute-start.3 = (f32[11,62,64]{2,0,1:T(8,128)S(1)}, f32[11,62,64]{2,0,1:T(8,128)}, u32[]{:S(2)}, u32[]{:S(2)}) collective-permute-start(f32[11,62,64]{2,0,1:T(8,128)S(1)} %maximum_maximum_fusion), channel_id=1, source_target_pairs={{4,0},{8,4},{12,8},{16,12},{20,16},{24,20},{28,24},{32,28},{36,32}... | collective-permute-start | bytes 523784 | tf_op jit(solution)/shard_map/ppermute | solution.py:24
  36.7 10.2 %all-to-all-start = ((f32[128,1,512]{2,1,0:T(1,128)}), f32[128,1,512]{2,1,0:T(1,128)}, u32[]{:S(2)}, u32[]{:S(2)}) async-start(f32[128,1,512]{2,1,0:T(1,128)} %reshape.5162), calls=%async_computation | async-start | bytes 524288 | tf_op jit(solution)/shard_map/all_to_all | solution.py:145
  49.6 7.0 %collective-permute-start.1 = (f32[11,768]{1,0:T(8,128)}, f32[11,768]{1,0:T(8,128)}, u32[]{:S(2)}, u32[]{:S(2)}) collective-permute-start(f32[11,768]{1,0:T(8,128)} %get-tuple-element.106), channel_id=1, source_target_pairs={{4,0},{8,4},{12,8},{16,12},{20,16},{24,20},{28,24},{32,28},{36,32}... | collective-permute-start | bytes 101384 | tf_op jit(solution)/shard_map/ppermute | solution.py:24
  87.8 5.4 %divide_reduce_fusion = f32[128,64]{1,0:T(8,128)S(1)} fusion(f32[128,64]{1,0:T(8,128)S(1)} %bitcast.632, f32[128,64]{1,0:T(8,128)S(1)} %copy-done.9, f32[128,64]{1,0:T(8,128)S(1)} %bitcast.635, f32[128,64]{1,0:T(8,128)S(1)} %copy-done.11, f32[128,64]{1,0:T(8,128)S(1)} %bitcast.629, f32[128,64]{1,0:T(8,128)S(1)} %copy-done.7), kind=kLoop, calls=%fused_computation.49 | loop fusion | flops 6283264 | bytes 229376 | tf_op jit(solution)/shard_map/reduce_sum | solution.py:38
  93.3 6.4 %multiply_divide_fusion = f32[128,64,64]{2,1,0:T(8,128)} fusion(f32[128,64]{1,0:T(8,128)S(1)} %divide_reduce_fusion, f32[128,64]{1,0:T(8,128)S(1)} %bitcast.633, f32[128,64]{1,0:T(8,128)S(1)} %copy-done.9, f32[128,64]{1,0:T(8,128)S(1)} %bitcast.636, f32[128,64]{1,0:T(8,128)S(1)} %copy-done.11, f32[128,64]{1,0:T(8,128)S(1)} %bitcast.630, ...), kind=kLoop, calls=%fused_computation.47 | loop fusion | flops 6291456 | bytes 2326528 | tf_op jit(solution)/shard_map/div | solution.py:38
  109.4 241.7 %while.10 = (s32[]{:T(128)}, f32[32,8,256]{2,1,0:T(8,128)}, s32[32,6]{1,0:T(8,128)}, f32[11,38,256]{2,0,1:T(8,128)S(1)}, f32[32,6]{1,0:T(8,128)}, /*index=5*/f32...) while((s32[]{:T(128)}, f32[32,8,256]{2,1,0:T(8,128)}, s32[32,6]{1,0:T(8,128)}, ...), condition=%wide.region_1.2_spmd, body=%wide.region_0.1_spmd.sunk | while | flops 42104376 | bytes 440149 | solution.py:64
  114.1 2.8 fusion.866
  121.6 2.8 fusion.866
  129.2 2.8 fusion.866
  136.7 2.8 fusion.866
  144.3 2.8 fusion.866
  151.8 2.8 fusion.866
  166.9 2.8 fusion.866
  174.5 2.8 fusion.866
  182.0 2.8 fusion.866
  197.1 2.8 fusion.866
  212.2 2.8 fusion.866
  219.7 2.9 fusion.866
  234.8 2.8 fusion.866
  242.4 2.8 fusion.866
  249.9 2.8 fusion.866
  272.6 2.8 fusion.866
  280.2 2.8 fusion.866
  295.3 2.8 fusion.866
  302.9 2.8 fusion.866
  325.5 2.8 fusion.866
  333.1 2.8 fusion.866
  340.7 2.9 fusion.866
  412.3 11.2 %bitcast_reduce_fusion = f32[8,64,64]{2,0,1:T(8,128)S(1)} fusion(f32[128,64]{1,0:T(8,128)} %copy-done.27, f32[128,64]{1,0:T(8,128)S(1)} %bitcast.634, f32[128,64]{1,0:T(8,128)S(1)} %copy-done.10, f32[128,64]{1,0:T(8,128)S(1)} %bitcast.637, f32[128,64]{1,0:T(8,128)S(1)} %copy-done.12, f32[128,64]{1,0:T(8,128)S(1)} %bitcast.631, ...), kind=kOutput, calls=%fused_computation.131 | convolution fusion | flops 56655872 | bytes 622592 | tf_op jit(solution)/shard_map/qnr,nrs->qns/dot_general | solution.py:157
  423.6 5.1 %bitcast_reduce_fusion.1 = f32[8,32,64]{2,0,1:T(8,128)S(1)} fusion(f32[8,64,64]{2,0,1:T(8,128)S(1)} %bitcast_reduce_fusion, f32[64,64]{1,0:T(8,128)S(1)} %copy-done.55, f32[64,64]{1,0:T(8,128)S(1)} %bitcast.647, f32[64,64]{1,0:T(8,128)S(1)} %copy-done.16, f32[64,64]{1,0:T(8,128)S(1)} %bitcast.650, f32[64,64]{1,0:T(8,128)S(1)} %copy-done.18, ...), kind=kOutput, calls=%fused_computation.189 | convolution fusion | flops 28327936 | bytes 311296 | tf_op jit(solution)/shard_map/qnr,nrs->qns/dot_general | solution.py:157
  458.7 3.2 fusion.17
  (1092 shorter events, 331.2 us)
Async XLA Ops:
  0.9 33.5 %copy-start.158 = (f32[2,64]{1,0:T(2,128)}, f32[2,64]{1,0:T(2,128)S(1)}, u32[]{:S(2)}) copy-start(f32[2,64]{1,0:T(2,128)S(1)} %get-tuple-element.191) | copy-start | bytes 1540
  0.9 33.5 %copy-start.161 = (f32[2,64]{1,0:T(2,128)}, f32[2,64]{1,0:T(2,128)S(1)}, u32[]{:S(2)}) copy-start(f32[2,64]{1,0:T(2,128)S(1)} %get-tuple-element.192) | copy-start | bytes 1540
  0.9 33.5 %copy-start.164 = (f32[2,64]{1,0:T(2,128)}, f32[2,64]{1,0:T(2,128)S(1)}, u32[]{:S(2)}) copy-start(f32[2,64]{1,0:T(2,128)S(1)} %get-tuple-element.193) | copy-start | bytes 1540
  15.7 17.6 %copy-start.32 = (f32[3,16128]{1,0:T(4,128)S(1)}, f32[3,16128]{1,0:T(4,128)}, u32[]{:S(2)}) copy-start(f32[3,16128]{1,0:T(4,128)} %param.24) | copy-start | bytes 580612
  15.7 17.4 %copy-start.152 = (f32[4,2,64]{2,1,0:T(2,128)}, f32[4,2,64]{2,1,0:T(2,128)S(1)}, u32[]{:S(2)}) copy-start(f32[4,2,64]{2,1,0:T(2,128)S(1)} %broadcast_in_dim.228) | copy-start | bytes 6148
  15.7 17.4 %copy-start.154 = (f32[4,2,64]{2,1,0:T(2,128)}, f32[4,2,64]{2,1,0:T(2,128)S(1)}, u32[]{:S(2)}) copy-start(f32[4,2,64]{2,1,0:T(2,128)S(1)} %broadcast_in_dim.232) | copy-start | bytes 6148
  15.7 17.4 %copy-start.156 = (f32[4,2,64]{2,1,0:T(2,128)}, f32[4,2,64]{2,1,0:T(2,128)S(1)}, u32[]{:S(2)}) copy-start(f32[4,2,64]{2,1,0:T(2,128)S(1)} %broadcast_in_dim.230) | copy-start | bytes 6148
  17.7 29.3 %copy-start.2 = (f32[8,8192]{1,0:T(8,128)S(1)}, f32[8,8192]{1,0:T(8,128)}, u32[]{:S(2)}) copy-start(f32[8,8192]{1,0:T(8,128)} %param.19) | copy-start | bytes 786436
  17.7 29.3 %copy-start.20 = (f32[3,8192]{1,0:T(4,128)S(1)}, f32[3,8192]{1,0:T(4,128)}, u32[]{:S(2)}) copy-start(f32[3,8192]{1,0:T(4,128)} %param.20) | copy-start | bytes 294916
  17.7 333.3 %collective-permute-start.3 = (f32[11,62,64]{2,0,1:T(8,128)S(1)}, f32[11,62,64]{2,0,1:T(8,128)}, u32[]{:S(2)}, u32[]{:S(2)}) collective-permute-start(f32[11,62,64]{2,0,1:T(8,128)S(1)} %maximum_maximum_fusion), channel_id=1, source_target_pairs={{4,0},{8,4},{12,8},{16,12},{20,16},{24,20},{28,24},{32,28},{36,32}... | collective-permute-start | bytes 523784 | tf_op jit(solution)/shard_map/ppermute | solution.py:24
  31.2 320.7 %collective-permute-start.2 = (f32[11,62,64]{2,0,1:T(8,128)S(1)}, f32[11,62,64]{2,0,1:T(8,128)}, u32[]{:S(2)}, u32[]{:S(2)}) collective-permute-start(f32[11,62,64]{2,0,1:T(8,128)S(1)} %maximum_maximum_fusion), channel_id=1, source_target_pairs={{0,4},{4,8},{8,12},{12,16},{16,20},{20,24},{24,28},{28,32},{32,36}... | collective-permute-start | bytes 523784 | tf_op jit(solution)/shard_map/ppermute | solution.py:23
  33.5 32.1 %copy-start = (f32[3,252,64]{2,1,0:T(8,128)}, f32[3,252,64]{2,1,0:T(8,128)S(1)}, u32[]{:S(2)}) copy-start(f32[3,252,64]{2,1,0:T(8,128)S(1)} %reshape.4905) | copy-start | bytes 580612
  33.5 29.4 %copy-start.184 = (s32[32,3]{0,1:T(4,128)S(1)}, s32[32,3]{0,1:T(4,128)}, u32[]{:S(2)}) copy-start(s32[32,3]{0,1:T(4,128)} %param.25) | copy-start | bytes 1156
  33.5 30.7 %copy-start.185 = (s32[32,6]{0,1:T(8,128)S(1)}, s32[32,6]{0,1:T(8,128)}, u32[]{:S(2)}) copy-start(s32[32,6]{0,1:T(8,128)} %param.21) | copy-start | bytes 2308
  36.7 372.5 %all-to-all-start = ((f32[128,1,512]{2,1,0:T(1,128)}), f32[128,1,512]{2,1,0:T(1,128)}, u32[]{:S(2)}, u32[]{:S(2)}) async-start(f32[128,1,512]{2,1,0:T(1,128)} %reshape.5162), calls=%async_computation | async-start | bytes 524288 | tf_op jit(solution)/shard_map/all_to_all | solution.py:145
  47.0 33.8 %copy-start.1 = (f32[11,8192]{1,0:T(8,128)}, f32[11,8192]{1,0:T(8,128)S(1)}, u32[]{:S(2)}) copy-start(f32[11,8192]{1,0:T(8,128)S(1)} %constant_dynamic-update-slice_fusion) | copy-start | bytes 1081348
  47.7 58.5 %collective-permute-start = (f32[11,768]{1,0:T(8,128)}, f32[11,768]{1,0:T(8,128)}, u32[]{:S(2)}, u32[]{:S(2)}) collective-permute-start(f32[11,768]{1,0:T(8,128)} %get-tuple-element.105), channel_id=1, source_target_pairs={{0,4},{4,8},{8,12},{12,16},{16,20},{20,24},{24,28},{28,32},{32,36}... | collective-permute-start | bytes 101384 | tf_op jit(solution)/shard_map/ppermute | solution.py:23
  49.6 56.6 %collective-permute-start.1 = (f32[11,768]{1,0:T(8,128)}, f32[11,768]{1,0:T(8,128)}, u32[]{:S(2)}, u32[]{:S(2)}) collective-permute-start(f32[11,768]{1,0:T(8,128)} %get-tuple-element.106), channel_id=1, source_target_pairs={{4,0},{8,4},{12,8},{16,12},{20,16},{24,20},{28,24},{32,28},{36,32}... | collective-permute-start | bytes 101384 | tf_op jit(solution)/shard_map/ppermute | solution.py:24
  65.5 18.2 %copy-start.28 = (f32[32,64]{1,0:T(8,128)}, f32[32,64]{1,0:T(8,128)S(1)}, u32[]{:S(2)}) copy-start(f32[32,64]{1,0:T(8,128)S(1)} %get-tuple-element.117) | copy-start | bytes 24580
  65.5 20.5 %copy-start.30 = (f32[32,64]{1,0:T(8,128)}, f32[32,64]{1,0:T(8,128)S(1)}, u32[]{:S(2)}) copy-start(f32[32,64]{1,0:T(8,128)S(1)} %get-tuple-element.118) | copy-start | bytes 24580
  65.6 18.1 %copy-start.15 = (f32[64,64]{1,0:T(8,128)}, f32[64,64]{1,0:T(8,128)S(1)}, u32[]{:S(2)}) copy-start(f32[64,64]{1,0:T(8,128)S(1)} %get-tuple-element.123) | copy-start | bytes 49156
  65.6 18.1 %copy-start.17 = (f32[64,64]{1,0:T(8,128)}, f32[64,64]{1,0:T(8,128)S(1)}, u32[]{:S(2)}) copy-start(f32[64,64]{1,0:T(8,128)S(1)} %get-tuple-element.124) | copy-start | bytes 49156
  65.6 20.5 %copy-start.13 = (f32[64,64]{1,0:T(8,128)}, f32[64,64]{1,0:T(8,128)S(1)}, u32[]{:S(2)}) copy-start(f32[64,64]{1,0:T(8,128)S(1)} %get-tuple-element.122) | copy-start | bytes 49156
  351.1 22.9 %copy-start.224 = (pred[8]{0:T(512)(128)(4,1)S(1)}, pred[8]{0:T(512)(128)(4,1)}, u32[]{:S(2)}) copy-start(pred[8]{0:T(512)(128)(4,1)} %get-tuple-element.271) | copy-start | bytes 28
  351.1 23.6 %copy-start.223 = (pred[8]{0:T(512)(128)(4,1)S(1)}, pred[8]{0:T(512)(128)(4,1)}, u32[]{:S(2)}) copy-start(pred[8]{0:T(512)(128)(4,1)} %compare_and_fusion.9) | copy-start | bytes 28
  351.1 26.8 %copy-start.19 = (f32[11,16,64]{2,0,1:T(8,128)S(1)}, f32[11,16,64]{2,0,1:T(8,128)}, u32[]{:S(2)}) copy-start(f32[11,16,64]{2,0,1:T(8,128)} %slice.1348) | copy-start | bytes 135172
  433.6 17.1 %copy-start.160 = (f32[2,64]{1,0:T(2,128)S(1)}, f32[2,64]{1,0:T(2,128)}, u32[]{:S(2)}) copy-start(f32[2,64]{1,0:T(2,128)} %copy-done.158) | copy-start | bytes 1540
  433.6 17.1 %copy-start.163 = (f32[2,64]{1,0:T(2,128)S(1)}, f32[2,64]{1,0:T(2,128)}, u32[]{:S(2)}) copy-start(f32[2,64]{1,0:T(2,128)} %copy-done.161) | copy-start | bytes 1540
  433.6 17.1 %copy-start.166 = (f32[2,64]{1,0:T(2,128)S(1)}, f32[2,64]{1,0:T(2,128)}, u32[]{:S(2)}) copy-start(f32[2,64]{1,0:T(2,128)} %copy-done.164) | copy-start | bytes 1540
  433.6 17.1 %copy-start.209 = (f32[64]{0:T(128)S(1)}, f32[64]{0:T(128)}, u32[]{:S(2)}) copy-start(f32[64]{0:T(128)} %copy-done.208) | copy-start | bytes 772
  433.6 17.1 %copy-start.211 = (f32[64]{0:T(128)S(1)}, f32[64]{0:T(128)}, u32[]{:S(2)}) copy-start(f32[64]{0:T(128)} %copy-done.210) | copy-start | bytes 772
  433.6 17.1 %copy-start.213 = (f32[64]{0:T(128)S(1)}, f32[64]{0:T(128)}, u32[]{:S(2)}) copy-start(f32[64]{0:T(128)} %copy-done.212) | copy-start | bytes 772
  (231 other events, 1433.7 us)
